TPU v7x, 128 devices: a whole 4x4x4 slice. The times are simulated.
128 devices in a mesh: tok: 8 (over z, x_lo), head: 16 (over x_hi, y, core).
Axes of the slice: x: 4 (x_hi: 2, x_lo: 2; x = x_hi * 2 + x_lo), y: 4, z: 4, core: 2. Of those that a mesh axis runs over, the one named last changes fastest.
Arguments:
- block_states: bfloat16 [2048, 4096], P('tok', 'head'), may hold values from -24 to 24
- token_ids: int32 [2048], replicated, may hold values from 0 to 100351
- accept: int32 [2048], P('tok'), may hold values 0 or 1
- cache_lengths: int32 [8], replicated, may hold values from 1 to 5120, as said below
- cache_keys: bfloat16 [8192, 4096], P('tok', 'head'), may hold values from -300 to 300
- cache_values: bfloat16 [8192, 4096], P('tok', 'head'), may hold values from -6 to 6
- w_query: bfloat16 [4096, 4096], P(None, 'head'), may hold values from -0.09375 to 0.09375
- w_key: bfloat16 [4096, 4096], P(None, 'head'), may hold values from -0.09375 to 0.09375
- w_value: bfloat16 [4096, 4096], P(None, 'head'), may hold values from -0.09375 to 0.09375
- w_out: bfloat16 [4096, 4096], P('head'), may hold values from -0.09375 to 0.09375
- attn_gain: float32 [4096], replicated, may hold values from 0.25 to 1.75
- final_gain: float32 [4096], replicated, may hold values from 0.25 to 1.75
- embed: bfloat16 [100352, 4096], P('tok', 'head'), may hold values from -6 to 6
- lm_head: bfloat16 [100352, 4096], P(('tok', 'head')), may hold values from -0.25 to 0.25
Outputs:
- hiddens: bfloat16 [2048, 4096], P(('tok', 'head'))
- request_norms: float32 [8], replicated
- top_logits: float32 [2048], replicated
Inputs may be any that keep to these rules, and one draw needn't show every extreme that they name: `cache_lengths`: each request has 1 or more cached positions; the counts sum to 8192 and the largest is exactly 5120.
All inputs are finite; a program needn't handle non-finite values. No bound on the sum of `accept` on one device may be relied on, other than what follows from the above.
Results may differ from a plain program's by a relative error of at most 0.0068.
Values may be sent and summed in bfloat16 or wider, within the bound.
A program may use at most 192 MiB of HBM per device.

v0:
```python
import math
import jax
import jax.numpy as jnp
from jax import lax
from jax.sharding import PartitionSpec as P

HEAD_DIM = 128
EPSILON = 1e-06


def row_norm(values):
    return values * lax.rsqrt(jnp.mean(values * values, axis=-1, keepdims=True) + EPSILON)


def softmax_block(softmax_state, query_heads, key_block, value_block, valid_keys, score_scale):
    running_max, running_sum, running_acc = softmax_state
    scores = (
        jnp.einsum("qhd,khd->hqk", query_heads, key_block, preferred_element_type=jnp.float32)
        * score_scale
    )
    masked = jnp.where(valid_keys[None, None, :], scores, -1e30)
    new_max = jnp.maximum(running_max, jnp.max(masked, axis=-1))
    weights = jnp.where(valid_keys[None, None, :], jnp.exp(masked - new_max[:, :, None]), 0.0)
    factor = jnp.exp(running_max - new_max)
    running_sum = running_sum * factor + jnp.sum(weights, axis=-1)
    running_acc = running_acc * factor[:, :, None] + jnp.einsum(
        "hqk,khd->hqd", weights, value_block.astype(jnp.float32)
    )
    return (new_max, running_sum, running_acc)


def shards(
    block_states,
    token_ids,
    accept,
    cache_lengths,
    cache_keys,
    cache_values,
    w_query,
    w_key,
    w_value,
    w_out,
    attn_gain,
    final_gain,
    embed,
    lm_head,
):
    tok_index = lax.axis_index("tok")
    head_index = lax.axis_index("head")
    tok_count = lax.axis_size("tok")
    head_count = lax.axis_size("head")
    block_rows = block_states.shape[0]
    model_width = w_query.shape[0]
    local_width = w_query.shape[1]
    heads_here = local_width // HEAD_DIM
    share_rows = block_rows // head_count
    key_span = 512
    score_scale = 1.0 / math.sqrt(HEAD_DIM)
    offsets = jnp.cumsum(cache_lengths) - cache_lengths
    zero_rows = jnp.zeros((key_span, local_width), jnp.bfloat16)
    gathered_keys, gathered_values = (
        lax.all_gather(cache_keys, "tok", axis=0, tiled=True),
        lax.all_gather(cache_values, "tok", axis=0, tiled=True),
    )
    gathered_keys = jnp.concatenate([gathered_keys, zero_rows], axis=0)
    gathered_values = jnp.concatenate([gathered_values, zero_rows], axis=0)

    def attention(queries, key_rows, value_rows):
        query_heads = queries.reshape(block_rows, heads_here, HEAD_DIM)
        own_state = softmax_block(
            (
                jnp.full((heads_here, block_rows), -1e30, jnp.float32),
                jnp.zeros((heads_here, block_rows), jnp.float32),
                jnp.zeros((heads_here, block_rows, HEAD_DIM), jnp.float32),
            ),
            query_heads,
            key_rows.reshape(block_rows, heads_here, HEAD_DIM),
            value_rows.reshape(block_rows, heads_here, HEAD_DIM),
            jnp.ones((block_rows,), bool),
            score_scale,
        )
        request_begin = offsets[tok_index]
        request_length = cache_lengths[tok_index]
        block_count = (request_length + key_span - 1) // key_span

        def advance(turn_index, softmax_state):
            key_start = request_begin + turn_index * key_span
            key_block = lax.dynamic_slice_in_dim(gathered_keys, key_start, key_span, 0).reshape(
                key_span, heads_here, HEAD_DIM
            )
            value_block = lax.dynamic_slice_in_dim(gathered_values, key_start, key_span, 0).reshape(
                key_span, heads_here, HEAD_DIM
            )
            valid_keys = (
                turn_index * key_span + jnp.arange(key_span, dtype=jnp.int32) < request_length
            )
            return softmax_block(
                softmax_state, query_heads, key_block, value_block, valid_keys, score_scale
            )

        final_state = lax.fori_loop(0, block_count, advance, own_state)
        running_max, running_sum, running_acc = final_state
        result = running_acc / running_sum[:, :, None]
        return (
            jnp.transpose(result, (1, 0, 2)).reshape(block_rows, local_width).astype(jnp.bfloat16)
        )

    def run_layer(features):
        piece_cols = lax.all_gather(features, "head", axis=1, tiled=True)
        query_acc = jnp.dot(piece_cols, w_query, preferred_element_type=jnp.float32)
        key_acc = jnp.dot(piece_cols, w_key, preferred_element_type=jnp.float32)
        value_acc = jnp.dot(piece_cols, w_value, preferred_element_type=jnp.float32)
        own_rows = lax.dynamic_slice_in_dim(piece_cols, head_index * share_rows, share_rows, 0)
        residual = own_rows
        query_acc, key_acc, value_acc, residual = (query_acc, key_acc, value_acc, residual)
        attended = attention(
            query_acc.astype(jnp.bfloat16),
            key_acc.astype(jnp.bfloat16),
            value_acc.astype(jnp.bfloat16),
        )
        projected = lax.psum_scatter(
            jnp.dot(attended, w_out, preferred_element_type=jnp.float32),
            "head",
            scatter_dimension=0,
            tiled=True,
        )
        return (residual.astype(jnp.float32) + row_norm(projected) * attn_gain).astype(jnp.bfloat16)

    first_pass = run_layer(block_states)
    row_piece = lax.all_gather(first_pass, ("tok", "head"), axis=0, tiled=True)
    piece_rows = row_piece.shape[0]
    widened = row_piece.astype(jnp.float32)
    row_squares = jnp.sum(widened * widened, axis=-1)
    normed = (row_norm(widened) * final_gain).astype(jnp.bfloat16)
    logits = lax.dot_general(
        normed, lm_head, (((1,), (1,)), ((), ())), preferred_element_type=jnp.float32
    )
    best = jnp.max(logits, axis=1)
    owners = jnp.arange(piece_rows, dtype=jnp.int32) // block_rows
    one_hot = (owners[:, None] == jnp.arange(tok_count, dtype=jnp.int32)[None, :]).astype(
        jnp.float32
    )
    square_sums = jnp.dot(row_squares, one_hot, precision=lax.Precision.HIGHEST)
    top_local, square_sums = (best, square_sums)
    top_logits = lax.pmax(top_local, ("tok", "head"))
    request_norms = jnp.sqrt(square_sums / (block_rows * model_width))
    vocab_here = embed.shape[0]
    local_ids = token_ids - tok_index * vocab_here
    inside_vocab = (local_ids >= 0) & (local_ids < vocab_here)
    looked_up = jnp.take(embed, jnp.clip(local_ids, 0, vocab_here - 1), axis=0)
    looked_up = jnp.where(inside_vocab[:, None], looked_up, jnp.zeros_like(looked_up)).astype(
        jnp.float32
    )
    embedded = lax.psum_scatter(
        looked_up.astype(jnp.bfloat16), "tok", scatter_dimension=0, tiled=True
    )
    swapped = jnp.where((accept == 1)[:, None], embedded, block_states)
    hiddens = run_layer(swapped)
    return (hiddens, request_norms, top_logits)


def solution(mesh):
    placed = (
        P("tok", "head"),
        P(),
        P("tok"),
        P(),
        P("tok", "head"),
        P("tok", "head"),
        P(None, "head"),
        P(None, "head"),
        P(None, "head"),
        P("head", None),
        P(),
        P(),
        P("tok", "head"),
        P(("tok", "head"), None),
    )
    return jax.shard_map(
        shards,
        mesh=mesh,
        in_specs=placed,
        out_specs=(P(("tok", "head"), None), P(), P()),
        check_vma=False,
    )
```

profile of v0, /device:TPU:1, one launch (start us, length us, event | category | flops | bytes accessed | tf_op | source)
XLA Modules:
  0.0 832.7 jit_solution(10681744635398324091)
XLA Ops:
  9.6 10.3 %gather_fusion = bf16[2048,256]{1,0:T(8,128)(2,1)S(1)} fusion(bf16[12544,256]{1,0:T(8,128)(2,1)} %param.30, s32[2048]{0:T(1024)S(1)} %fusion.34), kind=kCustom, calls=%fused_computation | custom fusion | bytes 2105344 | tf_op jit(solution)/shard_map/jit(_take)/gather | solution.py:150
  19.9 2.4 select_select_fusion
  23.1 39.3 %reduce-scatter.4.cloned.1.call-done = bf16[256,256]{1,0:T(8,128)(2,1)} async-done(((bf16[2048,256]{1,0:T(8,128)(2,1)}), bf16[256,256]{1,0:T(8,128)(2,1)}) %reduce-scatter.4.cloned.1.call-update) | async-done | bytes 131088 | tf_op jit(solution)/shard_map/reduce_scatter | solution.py:154
  69.4 7.6 all-gather.12.cloned.1.call-done
  77.0 3.1 convolution_convert_fusion.2
  80.3 3.3 convolution_convert_fusion.1
  85.3 39.0 %all-gather.6.cloned.1.call-done = bf16[256,4096]{1,0:T(8,128)(2,1)} async-done(((bf16[256,256]{1,0:T(8,128)(2,1)}), bf16[256,4096]{1,0:T(8,128)(2,1)}) %all-gather.6.cloned.1.call-update) | async-done | bytes 2097168 | tf_op jit(solution)/shard_map/all_gather | solution.py:109
  124.3 3.3 convolution_convert_fusion.5
  129.0 85.2 %all-gather.8.cloned.1.call-done = bf16[8192,256]{0,1:T(8,128)(2,1)} async-done(((bf16[1024,256]{0,1:T(8,128)(2,1)}), bf16[8192,256]{0,1:T(8,128)(2,1)}) %all-gather.8.cloned.1.call-update) | async-done | bytes 4194320 | tf_op jit(solution)/shard_map/all_gather | solution.py:62
  214.2 4.6 concatenate.6
  218.8 87.8 %all-gather.10.cloned.1.call-done = bf16[8192,256]{0,1:T(8,128)(2,1)} async-done(((bf16[1024,256]{0,1:T(8,128)(2,1)}), bf16[8192,256]{0,1:T(8,128)(2,1)}) %all-gather.10.cloned.1.call-update) | async-done | bytes 4194320 | tf_op jit(solution)/shard_map/all_gather | solution.py:63
  306.6 4.6 concatenate.7
  311.2 3.8 while.29
  315.2 2.7 fusion.42
  318.4 3.1 convolution_convert_fusion.3
  321.9 3.8 while.28
  325.9 2.7 fusion.41
  328.6 102.6 %reduce-scatter.8.cloned.1.call-done = f32[16,4096]{1,0:T(8,128)} async-done(((f32[256,4096]{1,0:T(8,128)}), f32[16,4096]{1,0:T(8,128)}) %reduce-scatter.8.cloned.1.call-update) | async-done | bytes 262160 | tf_op jit(solution)/shard_map/reduce_scatter | solution.py:121
  432.3 82.7 %reduce-scatter.6.cloned.1.call-done = f32[16,4096]{1,0:T(8,128)} async-done(((f32[256,4096]{1,0:T(8,128)}), f32[16,4096]{1,0:T(8,128)}) %reduce-scatter.6.cloned.1.call-update) | async-done | bytes 262160 | tf_op jit(solution)/shard_map/reduce_scatter | solution.py:121
  518.2 214.2 %all-gather.14.cloned.1.call-done = bf16[2048,4096]{1,0:T(8,128)(2,1)} async-done(((bf16[16,4096]{1,0:T(8,128)(2,1)}), bf16[2048,4096]{1,0:T(8,128)(2,1)}) %all-gather.14.cloned.1.call-update) | async-done | bytes 16777232 | tf_op jit(solution)/shard_map/all_gather | solution.py:130
  732.4 7.5 fusion.14
  740.0 3.1 copy-done.4
  743.1 17.2 %fusion.21 = f32[2048]{0:T(1024)S(1)} fusion(bf16[784,4096]{1,0:T(8,128)(2,1)} %param.31, bf16[2048,4096]{1,0:T(8,128)(2,1)S(1)} %copy-done.4, f32[4096]{0:T(1024)S(1)} %copy-done.10, f32[2048]{0:T(1024)S(1)} %add_rsqrt_fusion), kind=kOutput, calls=%fused_computation.39 | convolution fusion | flops 13188495360 | bytes 23232512 | tf_op jit(solution)/shard_map/dot_general | solution.py:135
  760.3 63.8 %pmax.7 = f32[2048]{0:T(1024)} all-reduce(f32[2048]{0:T(1024)S(1)} %fusion.21), channel_id=1, replica_groups=mesh['tok'=8,'head'=16] {'tok','head'}, use_global_device_ids=true, to_apply=%region_20.21 | all-reduce | flops 2048 | bytes 16384 | tf_op jit(solution)/shard_map/pmax | solution.py:145
  (93 shorter events, 24.5 us)
Async XLA Ops:
  8.0 307.2 %copy-start = (bf16[256,4096]{1,0:T(8,128)(2,1)S(1)}, bf16[256,4096]{1,0:T(8,128)(2,1)}, u32[]{:S(2)}) copy-start(bf16[256,4096]{1,0:T(8,128)(2,1)} %param.27) | copy-start | bytes 6291460
  8.0 54.4 %reduce-scatter.4.cloned.1.call-start = ((), (), s32[]{:S(2)}) async-start(), calls=%async_computation.3 | async-start | bytes 1179648 | tf_op jit(solution)/shard_map/reduce_scatter | solution.py:154
  19.9 3.1 copy-start.11
  19.9 42.4 %copy-start.8 = (bf16[256,256]{1,0:T(8,128)(2,1)S(1)}, bf16[256,256]{1,0:T(8,128)(2,1)}, u32[]{:S(2)}) copy-start(bf16[256,256]{1,0:T(8,128)(2,1)} %param.18) | copy-start | bytes 393220
  22.4 43.9 %copy-start.7 = (bf16[1024,256]{1,0:T(8,128)(2,1)S(1)}, bf16[1024,256]{1,0:T(8,128)(2,1)}, u32[]{:S(2)}) copy-start(bf16[1024,256]{1,0:T(8,128)(2,1)} %param.23) | copy-start | bytes 1572868
  22.4 44.9 %copy-start.12 = (s32[8]{0:T(128)S(1)}, s32[8]{0:T(128)}, u32[]{:S(2)}) copy-start(s32[8]{0:T(128)} %param.21) | copy-start | bytes 100
  22.4 54.6 %all-gather.12.cloned.1.call-start = ((), (), s32[]{:S(2)}) async-start(), calls=%async_computation.8 | async-start | bytes 2228224 | tf_op jit(solution)/shard_map/all_gather | solution.py:109
  23.0 101.3 %all-gather.6.cloned.1.call-start = ((), (), s32[]{:S(2)}) async-start(), calls=%async_computation.4 | async-start | bytes 2228224 | tf_op jit(solution)/shard_map/all_gather | solution.py:109
  64.1 150.1 %all-gather.8.cloned.1.call-start = ((), (), s32[]{:S(2)}) async-start(), calls=%async_computation.5 | async-start | bytes 4718592 | tf_op jit(solution)/shard_map/all_gather | solution.py:62
  66.2 240.4 %all-gather.10.cloned.1.call-start = ((), (), s32[]{:S(2)}) async-start(), calls=%async_computation.6 | async-start | bytes 4718592 | tf_op jit(solution)/shard_map/all_gather | solution.py:63
  67.3 364.0 %reduce-scatter.8.cloned.1.call-start = ((), (), s32[]{:S(2)}) async-start(), calls=%async_computation.9 | async-start | bytes 4456448 | tf_op jit(solution)/shard_map/reduce_scatter | solution.py:121
  80.3 3.7 copy-start.2
  80.3 3.7 copy-start.6
  124.3 3.3 copy-start.3
  124.3 3.5 copy-start.5
  318.0 197.1 %reduce-scatter.6.cloned.1.call-start = ((), (), s32[]{:S(2)}) async-start(), calls=%async_computation.7 | async-start | bytes 4456448 | tf_op jit(solution)/shard_map/reduce_scatter | solution.py:121
  328.6 187.6 %copy-start.9 = (f32[4096]{0:T(1024)S(1)}, f32[4096]{0:T(1024)}, u32[]{:S(2)}) copy-start(f32[4096]{0:T(1024)} %param.28) | copy-start | bytes 49156
  328.6 403.8 %all-gather.14.cloned.1.call-start = ((), (), s32[]{:S(2)}) async-start(), calls=%async_computation.10 | async-start | bytes 16908288 | tf_op jit(solution)/shard_map/all_gather | solution.py:130
  518.2 221.8 %copy-start.10 = (f32[4096]{0:T(1024)S(1)}, f32[4096]{0:T(1024)}, u32[]{:S(2)}) copy-start(f32[4096]{0:T(1024)} %param.29) | copy-start | bytes 49156
  732.4 10.7 %copy-start.4 = (bf16[2048,4096]{1,0:T(8,128)(2,1)S(1)}, bf16[2048,4096]{1,0:T(8,128)(2,1)}, u32[]{:S(2)}) copy-start(bf16[2048,4096]{1,0:T(8,128)(2,1)} %all-gather.14.cloned.1.call-done) | copy-start | bytes 50331652
  743.1 82.2 %copy-start.1 = (bf16[256,4096]{1,0:T(8,128)(2,1)S(1)}, bf16[256,4096]{1,0:T(8,128)(2,1)}, u32[]{:S(2)}) copy-start(bf16[256,4096]{1,0:T(8,128)(2,1)} %param.27) | copy-start | bytes 6291460
Sparse Core Ops, SparseCore 0:
  22.5 39.8 reduce-scatter.3
  518.3 214.0 all-gather.13
Sparse Core Ops, SparseCore 1:
  25.2 51.8 all-gather.11
  79.7 44.5 all-gather.5
  125.8 88.3 all-gather.7
  215.9 90.7 all-gather.9
  318.0 113.1 reduce-scatter.7
  435.8 79.2 reduce-scatter.5
where the time goes:
time: 834 us; the launch traced here: 833 us
  waiting for transfers between devices  659 us (79%)
  blocking collectives  63.8 us (8%)
  matrix products  41.5 us (5%)
  local copies, waits for them, and re-layouts  30.3 us (4%)
  other arithmetic  19.6 us (2%)
  between operations  16.6 us (2%)
    all_gather x1, waiting for transfers between devices, shards(): row_piece = lax.all_gather(first_pass, ('tok', 'head'), axis=0, tiled=True)  214 us
    reduce_scatter x2, waiting for transfers between devices, run_layer(): lax.psum_scatter(jnp.dot(attended, w_out, preferred_element_type=jnp.floa...  185 us
    all_gather x1, waiting for transfers between devices, shards(): lax.all_gather(cache_values, 'tok', axis=0, tiled=True)  87.8 us
    all_gather x1, waiting for transfers between devices, shards(): lax.all_gather(cache_keys, 'tok', axis=0, tiled=True)  85.2 us
    pmax x1, blocking collectives, shards(): top_logits = lax.pmax(top_local, ('tok', 'head'))  63.8 us
    all_gather x2, waiting for transfers between devices, run_layer(): piece_cols = lax.all_gather(features, 'head', axis=1, tiled=True)  46.6 us
    reduce_scatter x1, waiting for transfers between devices, shards(): lax.psum_scatter(looked_up.astype(jnp.bfloat16), 'tok', scatter_dimension...  39.3 us
    dot_general x1, matrix products, shards(): lax.dot_general(normed, lm_head, (((1,), (1,)), ((), ())), preferred_elem...  17.2 us
  transfers between devices with their start and end apart: 8, of which 8 were waited for; matrix products, arithmetic and copies ran while one was open for 4% of the time, Pallas kernels for 0%

commit v1 on v0

--- a/solution.py
+++ b/solution.py
@@ -60,7 +60,9 @@
     zero_rows = jnp.zeros((key_span, local_width), jnp.bfloat16)
     gathered_keys, gathered_values = (
         lax.all_gather(cache_keys, "tok", axis=0, tiled=True),
-        lax.all_gather(cache_values, "tok", axis=0, tiled=True),
+        jnp.concatenate(
+            lax.all_to_all(jnp.stack([cache_values] * lax.axis_size("tok")), "tok", 0, 0), axis=0
+        ),
     )
     gathered_keys = jnp.concatenate([gathered_keys, zero_rows], axis=0)
     gathered_values = jnp.concatenate([gathered_values, zero_rows], axis=0)

time: 834 us -> 746 us (0.89)
  waiting for transfers between devices: 659 us -> 552 us
  local copies, waits for them, and re-layouts: 30.3 us -> 44.9 us
    all_gather x1 -> x0, waiting for transfers between devices: 87.8 us -> none  [shards(): lax.all_gather(cache_values, 'tok', axis=0, tiled=True)]
    all_gather x2, waiting for transfers between devices: 46.6 us -> 0.03 us  [run_layer(): piece_cols = lax.all_gather(features, 'head', axis=1, tiled=True)]
    all_to_all x0 -> x1, waiting for transfers between devices: none -> 39.5 us  [shards(): lax.all_to_all(jnp.stack([cache_values] * lax.axis_size('tok')), 'tok', 0...]
    all_gather x1, waiting for transfers between devices: 85.2 us -> 73.4 us  [shards(): lax.all_gather(cache_keys, 'tok', axis=0, tiled=True)]
  transfers between devices with their start and end apart: 8 -> 8, of which waited for: 8 -> 6; matrix products, arithmetic and copies ran while one was open for 4% -> 7% of each run, Pallas kernels for 0% -> 0%
where the time goes in v1:
time: 746 us; the launch traced here: 745 us
  waiting for transfers between devices  552 us (74%)
  blocking collectives  63.8 us (9%)
  local copies, waits for them, and re-layouts  44.9 us (6%)
  matrix products  41.7 us (6%)
  other arithmetic  19.6 us (3%)
  between operations  16.7 us (2%)
    all_gather x1, waiting for transfers between devices, shards(): row_piece = lax.all_gather(first_pass, ('tok', 'head'), axis=0, tiled=True)  214 us
    reduce_scatter x2, waiting for transfers between devices, run_layer(): lax.psum_scatter(jnp.dot(attended, w_out, preferred_element_type=jnp.floa...  185 us
    all_gather x1, waiting for transfers between devices, shards(): lax.all_gather(cache_keys, 'tok', axis=0, tiled=True)  73.4 us
    pmax x1, blocking collectives, shards(): top_logits = lax.pmax(top_local, ('tok', 'head'))  63.8 us
    all_to_all x1, waiting for transfers between devices, shards(): lax.all_to_all(jnp.stack([cache_values] * lax.axis_size('tok')), 'tok', 0...  39.5 us
    reduce_scatter x1, waiting for transfers between devices, shards(): lax.psum_scatter(looked_up.astype(jnp.bfloat16), 'tok', scatter_dimension...  39.3 us
    dot_general x1, matrix products, shards(): lax.dot_general(normed, lm_head, (((1,), (1,)), ((), ())), preferred_elem...  17.2 us
  transfers between devices with their start and end apart: 8, of which 6 were waited for; matrix products, arithmetic and copies ran while one was open for 7% of the time, Pallas kernels for 0%

profile of v1, /device:TPU:1, one launch (start us, length us, event | category | flops | bytes accessed | tf_op | source)
XLA Modules:
  0.0 744.8 jit_solution(68889332668762787)
XLA Ops:
  9.6 10.3 %gather_fusion = bf16[2048,256]{1,0:T(8,128)(2,1)S(1)} fusion(bf16[12544,256]{1,0:T(8,128)(2,1)} %param.30, s32[2048]{0:T(1024)S(1)} %fusion.34), kind=kCustom, calls=%fused_computation | custom fusion | bytes 2105344 | tf_op jit(solution)/shard_map/jit(_take)/gather | solution.py:152
  23.1 39.3 %reduce-scatter.4.cloned.1.call-done = bf16[256,256]{1,0:T(8,128)(2,1)} async-done(((bf16[2048,256]{1,0:T(8,128)(2,1)}), bf16[256,256]{1,0:T(8,128)(2,1)}) %reduce-scatter.4.cloned.1.call-update) | async-done | bytes 131088 | tf_op jit(solution)/shard_map/reduce_scatter | solution.py:156
  68.9 4.7 all-to-all-start
  75.7 39.5 %all-to-all-done = bf16[8,1024,256]{1,2,0:T(8,128)(2,1)} async-done(((bf16[8,1024,256]{1,2,0:T(8,128)(2,1)}), bf16[8,1024,256]{1,2,0:T(8,128)(2,1)}, u32[]{:S(2)}, u32[]{:S(2)}) %all-to-all-start) | async-done | bytes 4194336 | tf_op jit(solution)/shard_map/all_to_all | solution.py:64
  115.2 6.4 copy.81
  121.6 6.4 copy.106
  128.0 4.7 concatenate.7.clone
  132.7 3.1 convolution_convert_fusion.2
  136.0 3.5 convolution_convert_fusion.1
  141.3 3.3 convolution_convert_fusion.5
  146.0 73.4 %all-gather.7.cloned.1.call-done = bf16[8192,256]{0,1:T(8,128)(2,1)} async-done(((bf16[1024,256]{0,1:T(8,128)(2,1)}), bf16[8192,256]{0,1:T(8,128)(2,1)}) %all-gather.7.cloned.1.call-update) | async-done | bytes 4194320 | tf_op jit(solution)/shard_map/all_gather | solution.py:62
  219.4 4.6 concatenate.6
  224.0 3.7 while.29
  227.9 2.7 fusion.42
  231.1 3.1 convolution_convert_fusion.3
  234.6 3.7 while.28
  238.5 2.7 fusion.41
  241.2 102.0 %reduce-scatter.8.cloned.1.call-done = f32[16,4096]{1,0:T(8,128)} async-done(((f32[256,4096]{1,0:T(8,128)}), f32[16,4096]{1,0:T(8,128)}) %reduce-scatter.8.cloned.1.call-update) | async-done | bytes 262160 | tf_op jit(solution)/shard_map/reduce_scatter | solution.py:123
  344.4 82.8 %reduce-scatter.6.cloned.1.call-done = f32[16,4096]{1,0:T(8,128)} async-done(((f32[256,4096]{1,0:T(8,128)}), f32[16,4096]{1,0:T(8,128)}) %reduce-scatter.6.cloned.1.call-update) | async-done | bytes 262160 | tf_op jit(solution)/shard_map/reduce_scatter | solution.py:123
  430.3 214.2 %all-gather.11.cloned.1.call-done = bf16[2048,4096]{1,0:T(8,128)(2,1)} async-done(((bf16[16,4096]{1,0:T(8,128)(2,1)}), bf16[2048,4096]{1,0:T(8,128)(2,1)}) %all-gather.11.cloned.1.call-update) | async-done | bytes 16777232 | tf_op jit(solution)/shard_map/all_gather | solution.py:132
  644.4 7.5 %fusion.14 = f32[2048]{0:T(1024)S(1)} fusion(bf16[2048,4096]{1,0:T(8,128)(2,1)} %all-gather.11.cloned.1.call-done), kind=kLoop, calls=%fused_computation.33 | loop fusion | flops 25163776 | bytes 16785408 | tf_op jit(solution)/shard_map/reduce_sum | solution.py:135
  652.0 3.1 copy-done.4
  655.1 17.2 %fusion.21 = f32[2048]{0:T(1024)S(1)} fusion(bf16[784,4096]{1,0:T(8,128)(2,1)} %param.31, bf16[2048,4096]{1,0:T(8,128)(2,1)S(1)} %copy-done.4, f32[4096]{0:T(1024)S(1)} %copy-done.10, f32[2048]{0:T(1024)S(1)} %add_rsqrt_fusion), kind=kOutput, calls=%fused_computation.39 | convolution fusion | flops 13188495360 | bytes 23232512 | tf_op jit(solution)/shard_map/dot_general | solution.py:137
  672.3 63.8 %pmax.7 = f32[2048]{0:T(1024)} all-reduce(f32[2048]{0:T(1024)S(1)} %fusion.21), channel_id=1, replica_groups=mesh['tok'=8,'head'=16] {'tok','head'}, use_global_device_ids=true, to_apply=%region_20.21 | all-reduce | flops 2048 | bytes 16384 | tf_op jit(solution)/shard_map/pmax | solution.py:147
  (95 shorter events, 28.6 us)
Async XLA Ops:
  8.0 219.9 %copy-start = (bf16[256,4096]{1,0:T(8,128)(2,1)S(1)}, bf16[256,4096]{1,0:T(8,128)(2,1)}, u32[]{:S(2)}) copy-start(bf16[256,4096]{1,0:T(8,128)(2,1)} %param.27) | copy-start | bytes 6291460
  8.0 54.3 %reduce-scatter.4.cloned.1.call-start = ((), (), s32[]{:S(2)}) async-start(), calls=%async_computation.4 | async-start | bytes 1179648 | tf_op jit(solution)/shard_map/reduce_scatter | solution.py:156
  19.9 3.1 copy-start.11
  19.9 42.4 %copy-start.8 = (bf16[256,256]{1,0:T(8,128)(2,1)S(1)}, bf16[256,256]{1,0:T(8,128)(2,1)}, u32[]{:S(2)}) copy-start(bf16[256,256]{1,0:T(8,128)(2,1)} %param.18) | copy-start | bytes 393220
  22.4 43.8 %copy-start.7 = (bf16[1024,256]{1,0:T(8,128)(2,1)S(1)}, bf16[1024,256]{1,0:T(8,128)(2,1)}, u32[]{:S(2)}) copy-start(bf16[1024,256]{1,0:T(8,128)(2,1)} %param.23) | copy-start | bytes 1572868
  22.4 110.3 %all-gather.9.cloned.1.call-start = ((), (), s32[]{:S(2)}) async-start(), calls=%async_computation.8 | async-start | bytes 2228224 | tf_op jit(solution)/shard_map/all_gather | solution.py:111
  23.0 118.3 %all-gather.5.cloned.1.call-start = ((), (), s32[]{:S(2)}) async-start(), calls=%async_computation.5 | async-start | bytes 2228224 | tf_op jit(solution)/shard_map/all_gather | solution.py:111
  64.0 155.3 %all-gather.7.cloned.1.call-start = ((), (), s32[]{:S(2)}) async-start(), calls=%async_computation.6 | async-start | bytes 4718592 | tf_op jit(solution)/shard_map/all_gather | solution.py:62
  68.9 4.7 copy-start.12
  68.9 46.2 %all-to-all-start = ((bf16[8,1024,256]{1,2,0:T(8,128)(2,1)}), bf16[8,1024,256]{1,2,0:T(8,128)(2,1)}, u32[]{:S(2)}, u32[]{:S(2)}) async-start(bf16[8,1024,256]{1,2,0:T(8,128)(2,1)} %stack.2), calls=%async_computation.1 | async-start | bytes 8388608 | tf_op jit(solution)/shard_map/all_to_all | solution.py:64
  73.6 269.6 %reduce-scatter.8.cloned.1.call-start = ((), (), s32[]{:S(2)}) async-start(), calls=%async_computation.9 | async-start | bytes 4456448 | tf_op jit(solution)/shard_map/reduce_scatter | solution.py:123
  136.0 3.9 copy-start.2
  136.0 3.9 copy-start.6
  141.2 3.3 copy-start.3
  141.3 3.5 copy-start.5
  230.6 196.5 %reduce-scatter.6.cloned.1.call-start = ((), (), s32[]{:S(2)}) async-start(), calls=%async_computation.7 | async-start | bytes 4456448 | tf_op jit(solution)/shard_map/reduce_scatter | solution.py:123
  241.2 187.1 %copy-start.9 = (f32[4096]{0:T(1024)S(1)}, f32[4096]{0:T(1024)}, u32[]{:S(2)}) copy-start(f32[4096]{0:T(1024)} %param.28) | copy-start | bytes 49156
  241.2 403.2 %all-gather.11.cloned.1.call-start = ((), (), s32[]{:S(2)}) async-start(), calls=%async_computation.10 | async-start | bytes 16908288 | tf_op jit(solution)/shard_map/all_gather | solution.py:132
  430.2 221.7 %copy-start.10 = (f32[4096]{0:T(1024)S(1)}, f32[4096]{0:T(1024)}, u32[]{:S(2)}) copy-start(f32[4096]{0:T(1024)} %param.29) | copy-start | bytes 49156
  644.4 10.7 %copy-start.4 = (bf16[2048,4096]{1,0:T(8,128)(2,1)S(1)}, bf16[2048,4096]{1,0:T(8,128)(2,1)}, u32[]{:S(2)}) copy-start(bf16[2048,4096]{1,0:T(8,128)(2,1)} %all-gather.11.cloned.1.call-done) | copy-start | bytes 50331652
  655.1 82.2 %copy-start.1 = (bf16[256,4096]{1,0:T(8,128)(2,1)S(1)}, bf16[256,4096]{1,0:T(8,128)(2,1)}, u32[]{:S(2)}) copy-start(bf16[256,4096]{1,0:T(8,128)(2,1)} %param.27) | copy-start | bytes 6291460
Sparse Core Ops, SparseCore 0:
  22.5 39.7 reduce-scatter.3
  430.4 214.0 all-gather.10
Sparse Core Ops, SparseCore 1:
  25.1 51.7 all-gather.8
  79.7 50.7 all-gather.4
  131.9 87.4 all-gather.6
  230.7 112.5 reduce-scatter.7
  347.8 79.2 reduce-scatter.5
